TPU v7x, 512 devices: a whole 4x8x8 slice. The times are simulated.
512 devices in a mesh: gs: 128 (over y, z, core), view: 4 (over x).
Axes of the slice: x: 4, y: 8, z: 8, core: 2. Of those that a mesh axis runs over, the one named last changes fastest.
Arguments:
- features: bfloat16 [131072, 128], P('gs'), may hold values from -6 to 6
- geometry: float32 [4, 9, 131072], P('view', None, 'gs'), as said below
- decoder: bfloat16 [128, 512], replicated, may hold values from -0.5 to 0.5
- teacher: bfloat16 [4, 131072, 512], P('view', 'gs'), may hold values from -3 to 3
- images: float32 [4, 3, 131072], P('view', None, 'gs'), may hold values from 0 to 1
- send_index: int32 [4, 128, 1024], P('view', 'gs'), may hold values from 0 to 1023, as said below
- tile_lists: int32 [4, 512, 8], P('view', 'gs'), may hold values from 0 to 7, as said below
- tile_lengths: int32 [4, 512], P('view', 'gs'), may hold values from 2 to 8
Outputs:
- feature_grad: float32 [131072, 128], P(('gs', 'view'))
- geometry_grad: float32 [4, 9, 131072], P('view', None, 'gs')
- decoder_grad: float32 [128, 512], replicated
Inputs may be any that keep to these rules, and one draw needn't show every extreme that they name: `send_index`: each row (one view, one source device) is a permutation of 0 .. 1023; positions k * 8 to (k + 1) * 8 - 1 hold the Gaussians sent to the device of gs index k. `tile_lists`: the 8 entries of a row are distinct. `geometry`: opacity logits lie in -7.5 .. -4, log conics between -2 log 16 and -2 log 16 + 2 log 4, shears in -2 .. 2, colors in 0 .. 1.
All inputs are finite; a program needn't handle non-finite values.
Results may differ from a plain program's by a relative error of at most 0.0017.
Values may be sent and summed in bfloat16 or wider, within the bound.
A program may use at most 64 MiB of HBM per device.

v0:
```python
import math
import jax
import jax.numpy as jnp
from jax import lax
from jax.sharding import PartitionSpec as P

FEAT = 128
CT = 512
TS = 16
BLK = 128
LIST = 8


def composite(tile_geo, alive_mask, pixel_x, pixel_y):
    delta_x = pixel_x[:, None] - tile_geo[0][None, :]
    delta_y = pixel_y[:, None] - tile_geo[1][None, :]
    conic_a = jnp.exp(tile_geo[2])
    conic_c = jnp.exp(tile_geo[3])
    conic_b = 0.8 * jnp.tanh(tile_geo[4]) * jnp.exp(0.5 * (tile_geo[2] + tile_geo[3]))
    exponent = -0.5 * (
        conic_a * delta_x * delta_x
        + 2.0 * conic_b * delta_x * delta_y
        + conic_c * delta_y * delta_y
    )
    opacity = alive_mask * jax.nn.sigmoid(tile_geo[5])
    alpha_val = opacity[None, :] * jnp.exp(exponent)
    log_keep = jnp.log1p(-alpha_val)
    pixel_count = pixel_x.shape[0]
    blocked = log_keep.reshape(pixel_count, LIST, BLK)
    inner = jnp.cumsum(blocked, axis=2) - blocked
    block_sums = jnp.sum(blocked, axis=2)
    outer = jnp.cumsum(block_sums, axis=1) - block_sums
    before = (inner + outer[:, :, None]).reshape(pixel_count, LIST * BLK)
    weights = alpha_val * jnp.exp(before)
    pixel_color = jnp.einsum("pi,ci->cp", weights, tile_geo[6:9], precision=lax.Precision.HIGHEST)
    return (weights, pixel_color)


def device_terms(
    recv_geo, recv_feat, decoder, teacher_dev, images_dev, lists, lengths, shard_index
):
    nblocks = recv_feat.shape[0] // BLK
    tile_pixels = TS * TS
    geo_blocks = recv_geo.reshape(9, nblocks, BLK)
    feat_blocks = recv_feat.reshape(nblocks, BLK, FEAT)
    within = jnp.arange(tile_pixels, dtype=jnp.int32)
    block_range = jnp.arange(nblocks, dtype=jnp.int32)
    slot_range = jnp.arange(LIST, dtype=jnp.int32)

    def tile_step(totals, tile_index):
        decoder_sum, geo_acc, feat_acc = totals
        block_ids = lists[tile_index]
        count = lengths[tile_index]
        alive_mask = jnp.broadcast_to(
            (slot_range < count).astype(jnp.float32)[:, None], (LIST, BLK)
        ).reshape(LIST * BLK)
        tile_geo = jnp.take(geo_blocks, block_ids, axis=1).reshape(9, LIST * BLK)
        feat_tile = jnp.take(feat_blocks, block_ids, axis=0).reshape(LIST * BLK, FEAT)
        column = 2 * TS * (shard_index % 30) + TS * (tile_index % 2) + within % TS
        row_index = 2 * TS * (shard_index // 30) + TS * (tile_index // 2) + within // TS
        pixel_x = column.astype(jnp.float32) + 0.5
        pixel_y = row_index.astype(jnp.float32) + 0.5
        (weights, pixel_color), pullback = jax.vjp(
            lambda geo_part: composite(geo_part, alive_mask, pixel_x, pixel_y), tile_geo
        )
        weight_b = weights.astype(jnp.bfloat16)
        rendered = jnp.dot(weight_b, feat_tile, preferred_element_type=jnp.float32).astype(
            jnp.bfloat16
        )
        pred = jnp.dot(rendered, decoder, preferred_element_type=jnp.float32)
        teacher_rows = lax.dynamic_slice_in_dim(
            teacher_dev, tile_index * tile_pixels, tile_pixels, 0
        )
        error_feat = pred - teacher_rows.astype(jnp.float32)
        gpred = (error_feat / jnp.sqrt(error_feat * error_feat + 0.04)).astype(jnp.bfloat16)
        grender = lax.dot_general(
            gpred, decoder, (((1,), (1,)), ((), ())), preferred_element_type=jnp.float32
        ).astype(jnp.bfloat16)
        decoder_sum = decoder_sum + lax.dot_general(
            rendered, gpred, (((0,), (0,)), ((), ())), preferred_element_type=jnp.float32
        )
        image_cols = lax.dynamic_slice_in_dim(images_dev, tile_index * tile_pixels, tile_pixels, 1)
        error_color = pixel_color - image_cols
        gcolor = error_color / jnp.sqrt(error_color * error_color + 0.04)
        gweight = lax.dot_general(
            grender, feat_tile, (((1,), (1,)), ((), ())), preferred_element_type=jnp.float32
        )
        gfeat_tile = lax.dot_general(
            weight_b, grender, (((0,), (0,)), ((), ())), preferred_element_type=jnp.float32
        )
        (ggeo_tile,) = pullback((gweight, gcolor))
        hits = (block_ids[:, None] == block_range[None, :]).astype(jnp.float32)
        geo_acc = geo_acc + jnp.einsum(
            "clb,ln->cnb", ggeo_tile.reshape(9, LIST, BLK), hits, precision=lax.Precision.HIGHEST
        )
        feat_acc = feat_acc + jnp.einsum(
            "ln,lbf->nbf",
            hits,
            gfeat_tile.reshape(LIST, BLK, FEAT),
            precision=lax.Precision.HIGHEST,
        )
        return ((decoder_sum, geo_acc, feat_acc), None)

    start_totals = (
        jnp.zeros((FEAT, CT), jnp.float32),
        jnp.zeros((9, nblocks, BLK), jnp.float32),
        jnp.zeros((nblocks, BLK, FEAT), jnp.float32),
    )
    tile_range = jnp.arange(lists.shape[0], dtype=jnp.int32)
    (decoder_sum, geo_acc, feat_acc), _ = lax.scan(tile_step, start_totals, tile_range)
    return (decoder_sum, geo_acc.reshape(9, nblocks * BLK), feat_acc.reshape(nblocks * BLK, FEAT))


def on_device(features, geometry, decoder, teacher, images, send_index, tile_lists, tile_lengths):
    send_order = send_index[0, 0]
    shard_index = lax.axis_index("gs")
    geo_send = jnp.take(geometry[0], send_order, axis=1)
    recv_geo = lax.all_to_all(geo_send, "gs", split_axis=1, concat_axis=1, tiled=True)
    feat_send = jnp.take(features, send_order, axis=0)
    recv_feat = lax.all_to_all(feat_send, "gs", split_axis=0, concat_axis=0, tiled=True)
    decoder_sum, geo_acc, feat_acc = device_terms(
        recv_geo,
        recv_feat,
        decoder,
        teacher[0],
        images[0],
        tile_lists[0],
        tile_lengths[0],
        shard_index,
    )
    returned_geo = lax.all_to_all(geo_acc, "gs", split_axis=1, concat_axis=1, tiled=True)
    returned_feat = lax.all_to_all(feat_acc, "gs", split_axis=0, concat_axis=0, tiled=True)
    geo_own = jnp.zeros_like(returned_geo).at[:, send_order].set(returned_geo)
    feat_own = jnp.zeros_like(returned_feat).at[send_order].set(returned_feat)
    quarter = feat_own.shape[0] // lax.axis_size("view")
    summed = lax.psum(feat_own, "view")
    feature_grad = lax.dynamic_slice_in_dim(summed, lax.axis_index("view") * quarter, quarter, 0)
    pixel_total = lax.axis_size("gs") * lax.axis_size("view") * tile_lists.shape[1] * TS * TS
    decoder_grad = lax.psum(decoder_sum, ("gs", "view")) * (1.0 / math.sqrt(pixel_total))
    return (feature_grad, geo_own[None], decoder_grad)


def solution(mesh):
    placed = (
        P("gs", None),
        P("view", None, "gs"),
        P(),
        P("view", "gs", None),
        P("view", None, "gs"),
        P("view", "gs", None),
        P("view", "gs", None),
        P("view", "gs"),
    )
    return jax.shard_map(
        on_device,
        mesh=mesh,
        in_specs=placed,
        out_specs=(P(("gs", "view"), None), P("view", None, "gs"), P()),
        check_vma=False,
    )
```

profile of v0, /device:TPU:8, one launch (start us, length us, event | category | flops | bytes accessed | tf_op | source)
XLA Modules:
  0.0 610.4 jit_solution(10011325874883574381)
XLA Ops:
  10.2 2.8 gather_fusion.2
  14.1 17.4 %all-to-all-start = ((f32[9,128,8]{0,2,1:T(8,128)}), f32[9,128,8]{0,2,1:T(8,128)S(1)}, u32[]{:S(2)}, u32[]{:S(2)}) async-start(f32[9,128,8]{0,2,1:T(8,128)} %bitcast_select_fusion.1), calls=%async_computation | async-start | bytes 1048576 | tf_op jit(solution)/shard_map/all_to_all | solution.py:118
  31.5 3.2 gather_fusion.3
  35.6 16.2 %all-to-all-done = f32[9,128,8]{0,2,1:T(8,128)S(1)} async-done(((f32[9,128,8]{0,2,1:T(8,128)}), f32[9,128,8]{0,2,1:T(8,128)S(1)}, u32[]{:S(2)}, u32[]{:S(2)}) %all-to-all-start) | async-done | bytes 36896 | tf_op jit(solution)/shard_map/all_to_all | solution.py:118
  51.8 6.5 %all-to-all-start.1 = ((bf16[128,8,128]{2,1,0:T(8,128)(2,1)}), bf16[128,8,128]{2,1,0:T(8,128)(2,1)S(1)}, u32[]{:S(2)}, u32[]{:S(2)}) async-start(bf16[128,8,128]{2,1,0:T(8,128)(2,1)} %bitcast_select_fusion.2), calls=%async_computation.1 | async-start | bytes 524288 | tf_op jit(solution)/shard_map/all_to_all | solution.py:120
  60.4 12.6 %all-to-all-done.1 = bf16[128,8,128]{2,1,0:T(8,128)(2,1)S(1)} async-done(((bf16[128,8,128]{2,1,0:T(8,128)(2,1)}), bf16[128,8,128]{2,1,0:T(8,128)(2,1)S(1)}, u32[]{:S(2)}, u32[]{:S(2)}) %all-to-all-start.1) | async-done | bytes 262176 | tf_op jit(solution)/shard_map/all_to_all | solution.py:120
  73.7 187.1 %while.21 = (s32[]{:T(128)}, f32[128,512]{1,0:T(8,128)}, f32[9,8,128]{2,1,0:T(8,128)}, f32[8,128,128]{2,0,1:T(8,128)}, s32[4]{0:T(128)S(1)}, /*index=5*/s32[4]{0...) while((s32[]{:T(128)}, f32[128,512]{1,0:T(8,128)}, ...), condition=%wide.region_13.14_spmd.clone.clone, body=%wide.region_0.13_spmd.clone.clone.sunk | while | flops 448201472 | bytes 62394652 | solution.py:110
  82.8 1.4 gather_fusion
  89.3 2.2 exponential_multiply_fusion.2
  91.6 1.1 fusion.164
  93.2 1.2 convert_bitcast_fusion.2
  95.6 1.4 rsqrt_multiply_fusion.2
  97.1 1.8 fusion.171
  98.9 1.2 multiply_convert_fusion.2
  101.7 1.2 convolution_add_fusion.8
  105.5 1.5 copy.140
  107.0 3.4 fusion.167
  110.4 1.5 copy.141
  114.7 2.3 fusion.168
  128.7 1.4 gather_fusion
  135.2 2.2 exponential_multiply_fusion.2
  137.5 1.1 fusion.164
  139.1 1.2 convert_bitcast_fusion.2
  141.6 1.4 rsqrt_multiply_fusion.2
  143.1 1.8 fusion.171
  144.9 1.2 multiply_convert_fusion.2
  147.6 2.3 convolution_add_fusion.8
  152.6 1.5 copy.140
  154.0 3.4 fusion.167
  157.4 1.5 copy.141
  161.7 2.3 fusion.168
  175.7 1.4 gather_fusion
  182.3 2.2 exponential_multiply_fusion.2
  186.2 1.2 convert_bitcast_fusion.2
  188.6 1.5 rsqrt_multiply_fusion.2
  190.1 1.8 fusion.171
  191.9 1.2 multiply_convert_fusion.2
  194.7 2.3 convolution_add_fusion.8
  199.6 1.5 copy.140
  201.1 3.4 fusion.167
  204.4 1.5 copy.141
  208.8 2.3 fusion.168
  222.8 1.4 gather_fusion
  229.3 2.2 exponential_multiply_fusion.2
  233.2 1.2 convert_bitcast_fusion.2
  235.6 1.5 rsqrt_multiply_fusion.2
  237.1 1.8 fusion.171
  239.0 1.2 multiply_convert_fusion.2
  241.7 2.3 convolution_add_fusion.8
  246.6 1.5 copy.140
  248.1 3.4 fusion.167
  251.5 1.5 copy.141
  255.8 2.3 fusion.168
  260.8 1.9 copy.80
  262.7 6.5 %all-to-all-start.2 = ((f32[128,8,128]{2,1,0:T(8,128)}), f32[128,8,128]{2,1,0:T(8,128)S(1)}, u32[]{:S(2)}, u32[]{:S(2)}) async-start(f32[128,8,128]{2,1,0:T(8,128)} %bitcast.11), calls=%async_computation.2 | async-start | bytes 1048576 | tf_op jit(solution)/shard_map/all_to_all | solution.py:132
  270.0 19.5 %all-to-all-done.2 = f32[128,8,128]{2,1,0:T(8,128)S(1)} async-done(((f32[128,8,128]{2,1,0:T(8,128)}), f32[128,8,128]{2,1,0:T(8,128)S(1)}, u32[]{:S(2)}, u32[]{:S(2)}) %all-to-all-start.2) | async-done | bytes 524320 | tf_op jit(solution)/shard_map/all_to_all | solution.py:132
  289.5 4.0 scatter_custom_fusion
  295.4 6.4 %all-to-all-start.3 = ((f32[9,128,8]{0,2,1:T(8,128)}), f32[9,128,8]{0,2,1:T(8,128)S(1)}, u32[]{:S(2)}, u32[]{:S(2)}) async-start(f32[9,128,8]{0,2,1:T(8,128)} %bitcast.13), calls=%async_computation.3 | async-start | bytes 1048576 | tf_op jit(solution)/shard_map/all_to_all | solution.py:131
  301.7 20.4 %all-to-all-done.3 = f32[9,128,8]{0,2,1:T(8,128)S(1)} async-done(((f32[9,128,8]{0,2,1:T(8,128)}), f32[9,128,8]{0,2,1:T(8,128)S(1)}, u32[]{:S(2)}, u32[]{:S(2)}) %all-to-all-start.3) | async-done | bytes 36896 | tf_op jit(solution)/shard_map/all_to_all | solution.py:131
  322.2 3.4 scatter_custom_fusion.1
  326.4 222.5 %all-reduce.14.cloned.1.call-done = f32[128,512]{1,0:T(8,128)} async-done(((f32[128,512]{1,0:T(8,128)}), f32[128,512]{1,0:T(8,128)}) %all-reduce.14.cloned.1.call-update) | async-done | bytes 262160 | tf_op jit(solution)/shard_map/psum | solution.py:139
  548.8 1.7 broadcast_multiply_fusion.2
  550.5 51.4 %all-reduce.12.cloned.1.call-done = f32[1024,128]{1,0:T(8,128)} async-done(((f32[1024,128]{1,0:T(8,128)}), f32[1024,128]{1,0:T(8,128)}) %all-reduce.12.cloned.1.call-update) | async-done | bytes 524304 | tf_op jit(solution)/shard_map/psum | solution.py:136
  602.0 1.6 constant_dynamic-slice_fusion.1
  (485 shorter events, 96.0 us)
Async XLA Ops:
  7.2 24.3 %copy-start = (bf16[1024,128]{1,0:T(8,128)(2,1)S(1)}, bf16[1024,128]{1,0:T(8,128)(2,1)}, u32[]{:S(2)}) copy-start(bf16[1024,128]{1,0:T(8,128)(2,1)} %param.10) | copy-start | bytes 786436
  14.1 37.7 %all-to-all-start = ((f32[9,128,8]{0,2,1:T(8,128)}), f32[9,128,8]{0,2,1:T(8,128)S(1)}, u32[]{:S(2)}, u32[]{:S(2)}) async-start(f32[9,128,8]{0,2,1:T(8,128)} %bitcast_select_fusion.1), calls=%async_computation | async-start | bytes 1048576 | tf_op jit(solution)/shard_map/all_to_all | solution.py:118
  51.8 21.3 %all-to-all-start.1 = ((bf16[128,8,128]{2,1,0:T(8,128)(2,1)}), bf16[128,8,128]{2,1,0:T(8,128)(2,1)S(1)}, u32[]{:S(2)}, u32[]{:S(2)}) async-start(bf16[128,8,128]{2,1,0:T(8,128)(2,1)} %bitcast_select_fusion.2), calls=%async_computation.1 | async-start | bytes 524288 | tf_op jit(solution)/shard_map/all_to_all | solution.py:120
  73.7 13.7 %copy-start.8 = (bf16[8,128,128]{2,1,0:T(8,128)(2,1)}, bf16[8,128,128]{2,1,0:T(8,128)(2,1)S(1)}, u32[]{:S(2)}) copy-start(bf16[8,128,128]{2,1,0:T(8,128)(2,1)S(1)} %get-tuple-element.843) | copy-start | bytes 786436 | tf_op jit(solution)/shard_map/while
  81.3 22.9 %copy-start.21 = (f32[256]{0:T(256)}, f32[256]{0:T(256)S(1)}, u32[]{:S(2)}) copy-start(f32[256]{0:T(256)S(1)} %get-tuple-element.768) | copy-start | bytes 3076 | tf_op jit(solution)/shard_map/while
  81.3 22.9 %copy-start.23 = (f32[256]{0:T(256)}, f32[256]{0:T(256)S(1)}, u32[]{:S(2)}) copy-start(f32[256]{0:T(256)S(1)} %get-tuple-element.765) | copy-start | bytes 3076 | tf_op jit(solution)/shard_map/while
  82.0 19.6 %copy-start.28 = (s32[8]{0:T(128)}, s32[8]{0:T(128)S(1)}, u32[]{:S(2)}) copy-start(s32[8]{0:T(128)S(1)} %get-tuple-element.785) | copy-start | bytes 100 | tf_op jit(solution)/shard_map/while
  84.2 18.9 %copy-start.5 = (f32[9,8,128]{2,0,1:T(8,128)}, f32[9,8,128]{2,0,1:T(8,128)S(1)}, u32[]{:S(2)}) copy-start(f32[9,8,128]{2,0,1:T(8,128)S(1)} %select_bitcast_fusion.2) | copy-start | bytes 110596 | tf_op jit(solution)/shard_map/while
  84.9 19.4 %copy-start.11 = (f32[1,8,128]{2,0,1:T(1,128)}, f32[1,8,128]{2,0,1:T(1,128)S(1)}, u32[]{:S(2)}) copy-start(f32[1,8,128]{2,0,1:T(1,128)S(1)} %get-tuple-element.769) | copy-start | bytes 12292 | tf_op jit(solution)/shard_map/while
  85.5 18.8 %copy-start.16 = (f32[1024]{0:T(1024)}, f32[1024]{0:T(1024)S(1)}, u32[]{:S(2)}) copy-start(f32[1024]{0:T(1024)S(1)} %bitcast_multiply_fusion.8) | copy-start | bytes 12292 | tf_op jit(solution)/shard_map/while
  111.9 2.1 copy-start.3
  114.7 2.3 copy-start.15
  114.7 2.3 copy-start.26
  114.7 2.4 copy-start.27
  114.7 3.3 copy-start.25
  117.0 2.6 copy-start.9
  119.6 13.7 %copy-start.8 = (bf16[8,128,128]{2,1,0:T(8,128)(2,1)}, bf16[8,128,128]{2,1,0:T(8,128)(2,1)S(1)}, u32[]{:S(2)}) copy-start(bf16[8,128,128]{2,1,0:T(8,128)(2,1)S(1)} %get-tuple-element.843) | copy-start | bytes 786436 | tf_op jit(solution)/shard_map/while
  127.3 24.0 %copy-start.21 = (f32[256]{0:T(256)}, f32[256]{0:T(256)S(1)}, u32[]{:S(2)}) copy-start(f32[256]{0:T(256)S(1)} %get-tuple-element.768) | copy-start | bytes 3076 | tf_op jit(solution)/shard_map/while
  127.3 24.0 %copy-start.23 = (f32[256]{0:T(256)}, f32[256]{0:T(256)S(1)}, u32[]{:S(2)}) copy-start(f32[256]{0:T(256)S(1)} %get-tuple-element.765) | copy-start | bytes 3076 | tf_op jit(solution)/shard_map/while
  128.0 19.6 %copy-start.28 = (s32[8]{0:T(128)}, s32[8]{0:T(128)S(1)}, u32[]{:S(2)}) copy-start(s32[8]{0:T(128)S(1)} %get-tuple-element.785) | copy-start | bytes 100 | tf_op jit(solution)/shard_map/while
  130.2 20.0 %copy-start.5 = (f32[9,8,128]{2,0,1:T(8,128)}, f32[9,8,128]{2,0,1:T(8,128)S(1)}, u32[]{:S(2)}) copy-start(f32[9,8,128]{2,0,1:T(8,128)S(1)} %select_bitcast_fusion.2) | copy-start | bytes 110596 | tf_op jit(solution)/shard_map/while
  130.8 20.5 %copy-start.11 = (f32[1,8,128]{2,0,1:T(1,128)}, f32[1,8,128]{2,0,1:T(1,128)S(1)}, u32[]{:S(2)}) copy-start(f32[1,8,128]{2,0,1:T(1,128)S(1)} %get-tuple-element.769) | copy-start | bytes 12292 | tf_op jit(solution)/shard_map/while
  131.4 19.9 %copy-start.16 = (f32[1024]{0:T(1024)}, f32[1024]{0:T(1024)S(1)}, u32[]{:S(2)}) copy-start(f32[1024]{0:T(1024)S(1)} %bitcast_multiply_fusion.8) | copy-start | bytes 12292 | tf_op jit(solution)/shard_map/while
  147.3 2.6 copy-start.7
  147.6 2.3 copy-start.4
  161.7 2.3 copy-start.15
  161.7 2.3 copy-start.26
  161.7 2.4 copy-start.27
  161.7 3.3 copy-start.25
  164.0 2.6 copy-start.9
  166.6 13.7 %copy-start.8 = (bf16[8,128,128]{2,1,0:T(8,128)(2,1)}, bf16[8,128,128]{2,1,0:T(8,128)(2,1)S(1)}, u32[]{:S(2)}) copy-start(bf16[8,128,128]{2,1,0:T(8,128)(2,1)S(1)} %get-tuple-element.843) | copy-start | bytes 786436 | tf_op jit(solution)/shard_map/while
  174.3 24.0 %copy-start.21 = (f32[256]{0:T(256)}, f32[256]{0:T(256)S(1)}, u32[]{:S(2)}) copy-start(f32[256]{0:T(256)S(1)} %get-tuple-element.768) | copy-start | bytes 3076 | tf_op jit(solution)/shard_map/while
  174.3 24.0 %copy-start.23 = (f32[256]{0:T(256)}, f32[256]{0:T(256)S(1)}, u32[]{:S(2)}) copy-start(f32[256]{0:T(256)S(1)} %get-tuple-element.765) | copy-start | bytes 3076 | tf_op jit(solution)/shard_map/while
  175.0 19.6 %copy-start.28 = (s32[8]{0:T(128)}, s32[8]{0:T(128)S(1)}, u32[]{:S(2)}) copy-start(s32[8]{0:T(128)S(1)} %get-tuple-element.785) | copy-start | bytes 100 | tf_op jit(solution)/shard_map/while
  177.2 20.0 %copy-start.5 = (f32[9,8,128]{2,0,1:T(8,128)}, f32[9,8,128]{2,0,1:T(8,128)S(1)}, u32[]{:S(2)}) copy-start(f32[9,8,128]{2,0,1:T(8,128)S(1)} %select_bitcast_fusion.2) | copy-start | bytes 110596 | tf_op jit(solution)/shard_map/while
  177.8 20.5 %copy-start.11 = (f32[1,8,128]{2,0,1:T(1,128)}, f32[1,8,128]{2,0,1:T(1,128)S(1)}, u32[]{:S(2)}) copy-start(f32[1,8,128]{2,0,1:T(1,128)S(1)} %get-tuple-element.769) | copy-start | bytes 12292 | tf_op jit(solution)/shard_map/while
  178.4 19.9 %copy-start.16 = (f32[1024]{0:T(1024)}, f32[1024]{0:T(1024)S(1)}, u32[]{:S(2)}) copy-start(f32[1024]{0:T(1024)S(1)} %bitcast_multiply_fusion.8) | copy-start | bytes 12292 | tf_op jit(solution)/shard_map/while
  194.3 2.6 copy-start.7
  194.6 2.3 copy-start.4
  205.9 2.1 copy-start.3
  208.7 2.3 copy-start.15
  208.7 2.3 copy-start.26
  208.7 2.4 copy-start.27
  208.7 3.3 copy-start.25
  211.0 2.6 copy-start.9
  213.7 13.7 %copy-start.8 = (bf16[8,128,128]{2,1,0:T(8,128)(2,1)}, bf16[8,128,128]{2,1,0:T(8,128)(2,1)S(1)}, u32[]{:S(2)}) copy-start(bf16[8,128,128]{2,1,0:T(8,128)(2,1)S(1)} %get-tuple-element.843) | copy-start | bytes 786436 | tf_op jit(solution)/shard_map/while
  221.3 24.0 %copy-start.21 = (f32[256]{0:T(256)}, f32[256]{0:T(256)S(1)}, u32[]{:S(2)}) copy-start(f32[256]{0:T(256)S(1)} %get-tuple-element.768) | copy-start | bytes 3076 | tf_op jit(solution)/shard_map/while
  221.3 24.0 %copy-start.23 = (f32[256]{0:T(256)}, f32[256]{0:T(256)S(1)}, u32[]{:S(2)}) copy-start(f32[256]{0:T(256)S(1)} %get-tuple-element.765) | copy-start | bytes 3076 | tf_op jit(solution)/shard_map/while
  222.0 19.6 %copy-start.28 = (s32[8]{0:T(128)}, s32[8]{0:T(128)S(1)}, u32[]{:S(2)}) copy-start(s32[8]{0:T(128)S(1)} %get-tuple-element.785) | copy-start | bytes 100 | tf_op jit(solution)/shard_map/while
  224.2 20.0 %copy-start.5 = (f32[9,8,128]{2,0,1:T(8,128)}, f32[9,8,128]{2,0,1:T(8,128)S(1)}, u32[]{:S(2)}) copy-start(f32[9,8,128]{2,0,1:T(8,128)S(1)} %select_bitcast_fusion.2) | copy-start | bytes 110596 | tf_op jit(solution)/shard_map/while
  224.9 20.5 %copy-start.11 = (f32[1,8,128]{2,0,1:T(1,128)}, f32[1,8,128]{2,0,1:T(1,128)S(1)}, u32[]{:S(2)}) copy-start(f32[1,8,128]{2,0,1:T(1,128)S(1)} %get-tuple-element.769) | copy-start | bytes 12292 | tf_op jit(solution)/shard_map/while
  225.5 19.9 %copy-start.16 = (f32[1024]{0:T(1024)}, f32[1024]{0:T(1024)S(1)}, u32[]{:S(2)}) copy-start(f32[1024]{0:T(1024)S(1)} %bitcast_multiply_fusion.8) | copy-start | bytes 12292 | tf_op jit(solution)/shard_map/while
  241.4 2.6 copy-start.7
  241.7 2.3 copy-start.4
  253.0 2.1 copy-start.3
  255.8 2.3 copy-start.15
  255.8 2.3 copy-start.26
  255.8 2.4 copy-start.27
  255.8 3.3 copy-start.25
  258.1 2.6 copy-start.9
  262.7 26.8 %all-to-all-start.2 = ((f32[128,8,128]{2,1,0:T(8,128)}), f32[128,8,128]{2,1,0:T(8,128)S(1)}, u32[]{:S(2)}, u32[]{:S(2)}) async-start(f32[128,8,128]{2,1,0:T(8,128)} %bitcast.11), calls=%async_computation.2 | async-start | bytes 1048576 | tf_op jit(solution)/shard_map/all_to_all | solution.py:132
  269.2 279.6 %all-reduce.14.cloned.1.call-start = ((), (), s32[]{:S(2)}) async-start(), calls=%async_computation.5 | async-start | bytes 524288 | tf_op jit(solution)/shard_map/psum | solution.py:139
  269.9 332.0 %all-reduce.12.cloned.1.call-start = ((), (), s32[]{:S(2)}) async-start(), calls=%async_computation.4 | async-start | bytes 1048576 | tf_op jit(solution)/shard_map/psum | solution.py:136
  295.4 26.8 %all-to-all-start.3 = ((f32[9,128,8]{0,2,1:T(8,128)}), f32[9,128,8]{0,2,1:T(8,128)S(1)}, u32[]{:S(2)}, u32[]{:S(2)}) async-start(f32[9,128,8]{0,2,1:T(8,128)} %bitcast.13), calls=%async_computation.3 | async-start | bytes 1048576 | tf_op jit(solution)/shard_map/all_to_all | solution.py:131
  (73 other events, 68.1 us)
Sparse Core Ops, SparseCore 0:
  275.6 273.1 all-reduce.13
  551.3 50.6 all-reduce.11
where the time goes:
time: 613 us; the launch traced here: 610 us
  waiting for transfers between devices  343 us (56%)
  local copies, waits for them, and re-layouts  79.9 us (13%)
  other arithmetic  76.6 us (12%)
  matrix products  39.1 us (6%)
  starting transfers between devices  36.8 us (6%)
  loops' own time  20.3 us (3%)
  between operations  14.3 us (2%)
    psum x1, waiting for transfers between devices, on_device(): lax.psum(decoder_sum, ('gs', 'view')) * (1.0 / math.sqrt(pixel_total))  222 us
    psum x1, waiting for transfers between devices, on_device(): summed = lax.psum(feat_own, 'view')  51.4 us
    another operation x8, other arithmetic, composite(): inner = jnp.cumsum(blocked, axis=2) - blocked  22.4 us
    all_to_all x1, waiting for transfers between devices, on_device(): lax.all_to_all(geo_acc, 'gs', split_axis=1, concat_axis=1, tiled=True)  20.4 us
    another operation x1, loops' own time, device_terms(): lax.scan(tile_step, start_totals, tile_range)  20.3 us
    all_to_all x1, waiting for transfers between devices, on_device(): lax.all_to_all(feat_acc, 'gs', split_axis=0, concat_axis=0, tiled=True)  19.5 us
    while x264, local copies, waits for them, and re-layouts  19.3 us
    all_to_all x1, starting transfers between devices, on_device(): lax.all_to_all(geo_send, 'gs', split_axis=1, concat_axis=1, tiled=True)  17.4 us
  transfers between devices with their start and end apart: 6, of which 6 were waited for; matrix products, arithmetic and copies ran while one was open for 3% of the time, Pallas kernels for 0%

commit v1 on v0

--- a/solution.py
+++ b/solution.py
@@ -136,7 +136,7 @@
     summed = lax.psum(feat_own, "view")
     feature_grad = lax.dynamic_slice_in_dim(summed, lax.axis_index("view") * quarter, quarter, 0)
     pixel_total = lax.axis_size("gs") * lax.axis_size("view") * tile_lists.shape[1] * TS * TS
-    decoder_grad = lax.psum(decoder_sum, ("gs", "view")) * (1.0 / math.sqrt(pixel_total))
+    decoder_grad = lax.psum(lax.psum(decoder_sum, "view"), "gs") * (1.0 / math.sqrt(pixel_total))
     return (feature_grad, geo_own[None], decoder_grad)
 
 

time: 613 us -> 546 us (0.89)
  the two profiles are of different devices: /device:TPU:8 before, /device:TPU:24 now
where the time goes in v1:
time: 546 us; the launch traced here: 543 us
  waiting for transfers between devices  254 us (47%)
  local copies, waits for them, and re-layouts  79.1 us (14%)
  other arithmetic  76.6 us (14%)
  matrix products  39.1 us (7%)
  starting transfers between devices  34 us (6%)
  blocking collectives  26 us (5%)
  loops' own time  20.3 us (4%)
  between operations  14.3 us (3%)
    psum x1, waiting for transfers between devices, on_device(): lax.psum(lax.psum(decoder_sum, 'view'), 'gs')  189 us
    psum x1, waiting for transfers between devices, on_device(): summed = lax.psum(feat_own, 'view')  39.8 us
    all_to_all x1, blocking collectives, on_device(): lax.all_to_all(feat_acc, 'gs', split_axis=0, concat_axis=0, tiled=True)  26 us
    another operation x8, other arithmetic, composite(): inner = jnp.cumsum(blocked, axis=2) - blocked  22.4 us
    another operation x1, loops' own time, device_terms(): lax.scan(tile_step, start_totals, tile_range)  20.3 us
    while x264, local copies, waits for them, and re-layouts  19.2 us
    all_to_all x1, starting transfers between devices, on_device(): lax.all_to_all(geo_send, 'gs', split_axis=1, concat_axis=1, tiled=True)  17.3 us
    dot_general x12, matrix products, composite(): jnp.einsum('pi,ci->cp', weights, tile_geo[6:9], precision=lax.Precision.H...  17.3 us
  transfers between devices with their start and end apart: 5, of which 4 were waited for; matrix products, arithmetic and copies ran while one was open for 2% of the time, Pallas kernels for 0%

profile of v1, /device:TPU:24, one launch (start us, length us, event | category | flops | bytes accessed | tf_op | source)
XLA Modules:
  0.0 543.4 jit_solution(13660900999529790537)
XLA Ops:
  10.2 2.8 gather_fusion.2
  14.1 17.3 %all-to-all-start = ((f32[9,128,8]{0,2,1:T(8,128)}), f32[9,128,8]{0,2,1:T(8,128)S(1)}, u32[]{:S(2)}, u32[]{:S(2)}) async-start(f32[9,128,8]{0,2,1:T(8,128)} %bitcast_select_fusion.1), calls=%async_computation | async-start | bytes 1048576 | tf_op jit(solution)/shard_map/all_to_all | solution.py:118
  31.4 3.2 gather_fusion.3
  35.6 14.3 %all-to-all-done = f32[9,128,8]{0,2,1:T(8,128)S(1)} async-done(((f32[9,128,8]{0,2,1:T(8,128)}), f32[9,128,8]{0,2,1:T(8,128)S(1)}, u32[]{:S(2)}, u32[]{:S(2)}) %all-to-all-start) | async-done | bytes 36896 | tf_op jit(solution)/shard_map/all_to_all | solution.py:118
  49.9 8.3 %all-to-all-start.1 = ((bf16[128,8,128]{2,1,0:T(8,128)(2,1)}), bf16[128,8,128]{2,1,0:T(8,128)(2,1)S(1)}, u32[]{:S(2)}, u32[]{:S(2)}) async-start(bf16[128,8,128]{2,1,0:T(8,128)(2,1)} %bitcast_select_fusion.2), calls=%async_computation.1 | async-start | bytes 524288 | tf_op jit(solution)/shard_map/all_to_all | solution.py:120
  60.4 10.9 %all-to-all-done.1 = bf16[128,8,128]{2,1,0:T(8,128)(2,1)S(1)} async-done(((bf16[128,8,128]{2,1,0:T(8,128)(2,1)}), bf16[128,8,128]{2,1,0:T(8,128)(2,1)S(1)}, u32[]{:S(2)}, u32[]{:S(2)}) %all-to-all-start.1) | async-done | bytes 262176 | tf_op jit(solution)/shard_map/all_to_all | solution.py:120
  72.0 187.1 %while.21 = (s32[]{:T(128)}, f32[128,512]{1,0:T(8,128)}, f32[9,8,128]{2,1,0:T(8,128)}, f32[8,128,128]{2,0,1:T(8,128)}, s32[4]{0:T(128)S(1)}, /*index=5*/s32[4]{0...) while((s32[]{:T(128)}, f32[128,512]{1,0:T(8,128)}, ...), condition=%wide.region_13.14_spmd.clone.clone, body=%wide.region_0.13_spmd.clone.clone.sunk | while | flops 448201472 | bytes 62394652 | solution.py:110
  81.1 1.4 gather_fusion
  87.6 2.2 exponential_multiply_fusion.2
  89.9 1.1 fusion.164
  91.5 1.2 convert_bitcast_fusion.2
  93.9 1.4 rsqrt_multiply_fusion.2
  95.4 1.8 fusion.171
  97.2 1.2 multiply_convert_fusion.2
  100.0 1.2 convolution_add_fusion.8
  103.8 1.5 copy.140
  105.3 3.4 fusion.167
  108.7 1.5 copy.141
  113.0 2.3 fusion.168
  127.0 1.4 gather_fusion
  133.6 2.2 exponential_multiply_fusion.2
  135.8 1.1 fusion.164
  137.4 1.2 convert_bitcast_fusion.2
  139.9 1.4 rsqrt_multiply_fusion.2
  141.4 1.8 fusion.171
  143.2 1.2 multiply_convert_fusion.2
  145.9 2.3 convolution_add_fusion.8
  150.9 1.5 copy.140
  152.3 3.4 fusion.167
  155.7 1.5 copy.141
  160.0 2.3 fusion.168
  174.0 1.4 gather_fusion
  180.6 2.2 exponential_multiply_fusion.2
  182.8 1.1 fusion.164
  184.5 1.2 convert_bitcast_fusion.2
  186.9 1.5 rsqrt_multiply_fusion.2
  188.4 1.8 fusion.171
  190.2 1.2 multiply_convert_fusion.2
  193.0 2.3 convolution_add_fusion.8
  197.9 1.5 copy.140
  199.4 3.4 fusion.167
  202.8 1.5 copy.141
  207.1 2.3 fusion.168
  221.1 1.4 gather_fusion
  227.6 2.2 exponential_multiply_fusion.2
  229.9 1.1 fusion.164
  231.5 1.2 convert_bitcast_fusion.2
  233.9 1.5 rsqrt_multiply_fusion.2
  235.4 1.8 fusion.171
  237.3 1.2 multiply_convert_fusion.2
  240.0 2.3 convolution_add_fusion.8
  244.9 1.5 copy.140
  246.4 3.4 fusion.167
  249.8 1.5 copy.141
  254.1 2.3 fusion.168
  259.1 1.1 copy.80
  260.2 26.0 %all_to_all.36 = f32[128,8,128]{2,1,0:T(8,128)S(1)} all-to-all(f32[128,8,128]{2,1,0:T(8,128)S(1)} %bitcast.322), channel_id=1, replica_groups=mesh['gs'=128,'view'=4] {'gs'}, dimensions={0} | all-to-all | bytes 1048576 | tf_op jit(solution)/shard_map/all_to_all | solution.py:132
  286.2 4.0 scatter_custom_fusion
  292.0 8.2 %all-to-all-start.3 = ((f32[9,128,8]{0,2,1:T(8,128)}), f32[9,128,8]{0,2,1:T(8,128)S(1)}, u32[]{:S(2)}, u32[]{:S(2)}) async-start(f32[9,128,8]{0,2,1:T(8,128)} %bitcast.13), calls=%async_computation.3 | async-start | bytes 1048576 | tf_op jit(solution)/shard_map/all_to_all | solution.py:131
  300.3 39.8 %all-reduce.15.cloned.1.call-done = (f32[1024,128]{1,0:T(8,128)}, f32[128,512]{1,0:T(8,128)}) async-done(((f32[1024,128]{1,0:T(8,128)}, f32[128,512]{1,0:T(8,128)}), (f32[1024,128]{1,0:T(8,128)}, f32[128,512]{1,0:T(8,128)})) %all-reduce.15.cloned.1.call-update) | async-done | bytes 786448 | tf_op jit(solution)/shard_map/psum | solution.py:136
  340.1 3.4 scatter_custom_fusion.1
  344.3 1.6 constant_dynamic-slice_fusion.1
  345.9 189.0 %all-reduce.13.cloned.1.call-done = f32[128,512]{1,0:T(8,128)} async-done(((f32[128,512]{1,0:T(8,128)}), f32[128,512]{1,0:T(8,128)}) %all-reduce.13.cloned.1.call-update) | async-done | bytes 262160 | tf_op jit(solution)/shard_map/psum | solution.py:139
  534.9 1.7 broadcast_multiply_fusion.2
  (484 shorter events, 93.2 us)
Async XLA Ops:
  7.2 24.3 %copy-start = (bf16[1024,128]{1,0:T(8,128)(2,1)S(1)}, bf16[1024,128]{1,0:T(8,128)(2,1)}, u32[]{:S(2)}) copy-start(bf16[1024,128]{1,0:T(8,128)(2,1)} %param.10) | copy-start | bytes 786436
  14.1 35.8 %all-to-all-start = ((f32[9,128,8]{0,2,1:T(8,128)}), f32[9,128,8]{0,2,1:T(8,128)S(1)}, u32[]{:S(2)}, u32[]{:S(2)}) async-start(f32[9,128,8]{0,2,1:T(8,128)} %bitcast_select_fusion.1), calls=%async_computation | async-start | bytes 1048576 | tf_op jit(solution)/shard_map/all_to_all | solution.py:118
  49.9 21.4 %all-to-all-start.1 = ((bf16[128,8,128]{2,1,0:T(8,128)(2,1)}), bf16[128,8,128]{2,1,0:T(8,128)(2,1)S(1)}, u32[]{:S(2)}, u32[]{:S(2)}) async-start(bf16[128,8,128]{2,1,0:T(8,128)(2,1)} %bitcast_select_fusion.2), calls=%async_computation.1 | async-start | bytes 524288 | tf_op jit(solution)/shard_map/all_to_all | solution.py:120
  58.2 281.9 %all-reduce.15.cloned.1.call-start = ((), (), s32[]{:S(2)}) async-start(), calls=%async_computation.5 | async-start | bytes 1572864 | tf_op jit(solution)/shard_map/psum | solution.py:136
  72.0 13.7 %copy-start.8 = (bf16[8,128,128]{2,1,0:T(8,128)(2,1)}, bf16[8,128,128]{2,1,0:T(8,128)(2,1)S(1)}, u32[]{:S(2)}) copy-start(bf16[8,128,128]{2,1,0:T(8,128)(2,1)S(1)} %get-tuple-element.845) | copy-start | bytes 786436 | tf_op jit(solution)/shard_map/while
  79.6 22.9 %copy-start.21 = (f32[256]{0:T(256)}, f32[256]{0:T(256)S(1)}, u32[]{:S(2)}) copy-start(f32[256]{0:T(256)S(1)} %get-tuple-element.770) | copy-start | bytes 3076 | tf_op jit(solution)/shard_map/while
  79.6 22.9 %copy-start.23 = (f32[256]{0:T(256)}, f32[256]{0:T(256)S(1)}, u32[]{:S(2)}) copy-start(f32[256]{0:T(256)S(1)} %get-tuple-element.767) | copy-start | bytes 3076 | tf_op jit(solution)/shard_map/while
  80.3 19.6 %copy-start.28 = (s32[8]{0:T(128)}, s32[8]{0:T(128)S(1)}, u32[]{:S(2)}) copy-start(s32[8]{0:T(128)S(1)} %get-tuple-element.787) | copy-start | bytes 100 | tf_op jit(solution)/shard_map/while
  82.5 18.9 %copy-start.5 = (f32[9,8,128]{2,0,1:T(8,128)}, f32[9,8,128]{2,0,1:T(8,128)S(1)}, u32[]{:S(2)}) copy-start(f32[9,8,128]{2,0,1:T(8,128)S(1)} %select_bitcast_fusion.2) | copy-start | bytes 110596 | tf_op jit(solution)/shard_map/while
  83.2 19.4 %copy-start.11 = (f32[1,8,128]{2,0,1:T(1,128)}, f32[1,8,128]{2,0,1:T(1,128)S(1)}, u32[]{:S(2)}) copy-start(f32[1,8,128]{2,0,1:T(1,128)S(1)} %get-tuple-element.771) | copy-start | bytes 12292 | tf_op jit(solution)/shard_map/while
  83.8 18.8 %copy-start.16 = (f32[1024]{0:T(1024)}, f32[1024]{0:T(1024)S(1)}, u32[]{:S(2)}) copy-start(f32[1024]{0:T(1024)S(1)} %bitcast_multiply_fusion.8) | copy-start | bytes 12292 | tf_op jit(solution)/shard_map/while
  110.2 2.1 copy-start.3
  113.0 2.3 copy-start.15
  113.0 2.3 copy-start.26
  113.0 2.4 copy-start.27
  113.0 3.3 copy-start.25
  115.3 2.6 copy-start.9
  117.9 13.7 %copy-start.8 = (bf16[8,128,128]{2,1,0:T(8,128)(2,1)}, bf16[8,128,128]{2,1,0:T(8,128)(2,1)S(1)}, u32[]{:S(2)}) copy-start(bf16[8,128,128]{2,1,0:T(8,128)(2,1)S(1)} %get-tuple-element.845) | copy-start | bytes 786436 | tf_op jit(solution)/shard_map/while
  125.6 24.0 %copy-start.21 = (f32[256]{0:T(256)}, f32[256]{0:T(256)S(1)}, u32[]{:S(2)}) copy-start(f32[256]{0:T(256)S(1)} %get-tuple-element.770) | copy-start | bytes 3076 | tf_op jit(solution)/shard_map/while
  125.6 24.0 %copy-start.23 = (f32[256]{0:T(256)}, f32[256]{0:T(256)S(1)}, u32[]{:S(2)}) copy-start(f32[256]{0:T(256)S(1)} %get-tuple-element.767) | copy-start | bytes 3076 | tf_op jit(solution)/shard_map/while
  126.3 19.6 %copy-start.28 = (s32[8]{0:T(128)}, s32[8]{0:T(128)S(1)}, u32[]{:S(2)}) copy-start(s32[8]{0:T(128)S(1)} %get-tuple-element.787) | copy-start | bytes 100 | tf_op jit(solution)/shard_map/while
  128.5 20.0 %copy-start.5 = (f32[9,8,128]{2,0,1:T(8,128)}, f32[9,8,128]{2,0,1:T(8,128)S(1)}, u32[]{:S(2)}) copy-start(f32[9,8,128]{2,0,1:T(8,128)S(1)} %select_bitcast_fusion.2) | copy-start | bytes 110596 | tf_op jit(solution)/shard_map/while
  129.1 20.5 %copy-start.11 = (f32[1,8,128]{2,0,1:T(1,128)}, f32[1,8,128]{2,0,1:T(1,128)S(1)}, u32[]{:S(2)}) copy-start(f32[1,8,128]{2,0,1:T(1,128)S(1)} %get-tuple-element.771) | copy-start | bytes 12292 | tf_op jit(solution)/shard_map/while
  129.7 19.9 %copy-start.16 = (f32[1024]{0:T(1024)}, f32[1024]{0:T(1024)S(1)}, u32[]{:S(2)}) copy-start(f32[1024]{0:T(1024)S(1)} %bitcast_multiply_fusion.8) | copy-start | bytes 12292 | tf_op jit(solution)/shard_map/while
  145.6 2.6 copy-start.7
  145.9 2.3 copy-start.4
  157.2 2.1 copy-start.3
  160.0 2.3 copy-start.15
  160.0 2.3 copy-start.26
  160.0 2.4 copy-start.27
  160.0 3.3 copy-start.25
  162.3 2.6 copy-start.9
  164.9 13.7 %copy-start.8 = (bf16[8,128,128]{2,1,0:T(8,128)(2,1)}, bf16[8,128,128]{2,1,0:T(8,128)(2,1)S(1)}, u32[]{:S(2)}) copy-start(bf16[8,128,128]{2,1,0:T(8,128)(2,1)S(1)} %get-tuple-element.845) | copy-start | bytes 786436 | tf_op jit(solution)/shard_map/while
  172.6 24.0 %copy-start.21 = (f32[256]{0:T(256)}, f32[256]{0:T(256)S(1)}, u32[]{:S(2)}) copy-start(f32[256]{0:T(256)S(1)} %get-tuple-element.770) | copy-start | bytes 3076 | tf_op jit(solution)/shard_map/while
  172.6 24.0 %copy-start.23 = (f32[256]{0:T(256)}, f32[256]{0:T(256)S(1)}, u32[]{:S(2)}) copy-start(f32[256]{0:T(256)S(1)} %get-tuple-element.767) | copy-start | bytes 3076 | tf_op jit(solution)/shard_map/while
  173.3 19.6 %copy-start.28 = (s32[8]{0:T(128)}, s32[8]{0:T(128)S(1)}, u32[]{:S(2)}) copy-start(s32[8]{0:T(128)S(1)} %get-tuple-element.787) | copy-start | bytes 100 | tf_op jit(solution)/shard_map/while
  175.5 20.0 %copy-start.5 = (f32[9,8,128]{2,0,1:T(8,128)}, f32[9,8,128]{2,0,1:T(8,128)S(1)}, u32[]{:S(2)}) copy-start(f32[9,8,128]{2,0,1:T(8,128)S(1)} %select_bitcast_fusion.2) | copy-start | bytes 110596 | tf_op jit(solution)/shard_map/while
  176.1 20.5 %copy-start.11 = (f32[1,8,128]{2,0,1:T(1,128)}, f32[1,8,128]{2,0,1:T(1,128)S(1)}, u32[]{:S(2)}) copy-start(f32[1,8,128]{2,0,1:T(1,128)S(1)} %get-tuple-element.771) | copy-start | bytes 12292 | tf_op jit(solution)/shard_map/while
  176.7 19.9 %copy-start.16 = (f32[1024]{0:T(1024)}, f32[1024]{0:T(1024)S(1)}, u32[]{:S(2)}) copy-start(f32[1024]{0:T(1024)S(1)} %bitcast_multiply_fusion.8) | copy-start | bytes 12292 | tf_op jit(solution)/shard_map/while
  192.6 2.6 copy-start.7
  193.0 2.3 copy-start.4
  204.2 2.1 copy-start.3
  207.0 2.3 copy-start.15
  207.0 2.3 copy-start.26
  207.0 2.4 copy-start.27
  207.1 3.3 copy-start.25
  209.3 2.6 copy-start.9
  212.0 13.7 %copy-start.8 = (bf16[8,128,128]{2,1,0:T(8,128)(2,1)}, bf16[8,128,128]{2,1,0:T(8,128)(2,1)S(1)}, u32[]{:S(2)}) copy-start(bf16[8,128,128]{2,1,0:T(8,128)(2,1)S(1)} %get-tuple-element.845) | copy-start | bytes 786436 | tf_op jit(solution)/shard_map/while
  219.6 24.0 %copy-start.21 = (f32[256]{0:T(256)}, f32[256]{0:T(256)S(1)}, u32[]{:S(2)}) copy-start(f32[256]{0:T(256)S(1)} %get-tuple-element.770) | copy-start | bytes 3076 | tf_op jit(solution)/shard_map/while
  219.6 24.0 %copy-start.23 = (f32[256]{0:T(256)}, f32[256]{0:T(256)S(1)}, u32[]{:S(2)}) copy-start(f32[256]{0:T(256)S(1)} %get-tuple-element.767) | copy-start | bytes 3076 | tf_op jit(solution)/shard_map/while
  220.3 19.6 %copy-start.28 = (s32[8]{0:T(128)}, s32[8]{0:T(128)S(1)}, u32[]{:S(2)}) copy-start(s32[8]{0:T(128)S(1)} %get-tuple-element.787) | copy-start | bytes 100 | tf_op jit(solution)/shard_map/while
  222.5 20.0 %copy-start.5 = (f32[9,8,128]{2,0,1:T(8,128)}, f32[9,8,128]{2,0,1:T(8,128)S(1)}, u32[]{:S(2)}) copy-start(f32[9,8,128]{2,0,1:T(8,128)S(1)} %select_bitcast_fusion.2) | copy-start | bytes 110596 | tf_op jit(solution)/shard_map/while
  223.2 20.5 %copy-start.11 = (f32[1,8,128]{2,0,1:T(1,128)}, f32[1,8,128]{2,0,1:T(1,128)S(1)}, u32[]{:S(2)}) copy-start(f32[1,8,128]{2,0,1:T(1,128)S(1)} %get-tuple-element.771) | copy-start | bytes 12292 | tf_op jit(solution)/shard_map/while
  223.8 19.9 %copy-start.16 = (f32[1024]{0:T(1024)}, f32[1024]{0:T(1024)S(1)}, u32[]{:S(2)}) copy-start(f32[1024]{0:T(1024)S(1)} %bitcast_multiply_fusion.8) | copy-start | bytes 12292 | tf_op jit(solution)/shard_map/while
  239.7 2.6 copy-start.7
  240.0 2.3 copy-start.4
  251.3 2.1 copy-start.3
  254.1 2.3 copy-start.15
  254.1 2.3 copy-start.26
  254.1 2.4 copy-start.27
  254.1 3.3 copy-start.25
  256.4 2.6 copy-start.9
  292.0 48.1 %all-to-all-start.3 = ((f32[9,128,8]{0,2,1:T(8,128)}), f32[9,128,8]{0,2,1:T(8,128)S(1)}, u32[]{:S(2)}, u32[]{:S(2)}) async-start(f32[9,128,8]{0,2,1:T(8,128)} %bitcast.13), calls=%async_computation.3 | async-start | bytes 1048576 | tf_op jit(solution)/shard_map/all_to_all | solution.py:131
  300.3 234.6 %all-reduce.13.cloned.1.call-start = ((), (), s32[]{:S(2)}) async-start(), calls=%async_computation.4 | async-start | bytes 524288 | tf_op jit(solution)/shard_map/psum | solution.py:139
  (72 other events, 65.9 us)
Sparse Core Ops, SparseCore 0:
  290.4 49.6 all-reduce.14
  343.3 191.5 all-reduce.12
